TPU v7x, 256 devices: a whole 4x4x8 slice. The times are simulated.
256 devices in a mesh: patch: 16 (over z_hi, x), wrow: 4 (over z_lo, core), wcol: 4 (over y).
Axes of the slice: x: 4, y: 4, z: 8 (z_hi: 4, z_lo: 2; z = z_hi * 2 + z_lo), core: 2. Of those that a mesh axis runs over, the one named last changes fastest.
Arguments:
- hidden_states: bfloat16 [4, 8192, 1536], P('wrow', ('patch', 'wcol')), may hold values from -6 to 6
- modulation: float32 [4, 3, 1536], P('wrow'), may hold values from -4 to 4
- w_qkv: bfloat16 [1536, 3, 1536], P('wrow', None, 'wcol'), may hold values from -1 to 1
- w_out: bfloat16 [1536, 1536], P('wcol', 'wrow'), may hold values from -0.15625 to 0.15625
- lengths: int32 [4], P('wrow'), may hold values from 1 to 8192, 20480 in all
Outputs:
- updated: bfloat16 [4, 8192, 1536], P('wrow', ('patch', 'wcol'))
Inputs may be any that keep to these rules, and one draw needn't show every extreme that they name: lengths[v] real tokens in video v, padding after them; the longest video fills all 8192 slots.
All inputs are finite; a program needn't handle non-finite values. No bound on the sum of `lengths` on one device may be relied on, other than what follows from the above.
Results may differ from a plain program's by a relative error of at most 0.015.
The roundings to bfloat16 on the way count: a program that leaves them out, or rounds other values in their place, can miss the bound.
Values may be sent and summed in bfloat16 or wider, within the bound.
A program may use at most 64 MiB of HBM per device.

v0:
```python
import jax
import jax.numpy as jnp
from jax import lax
from jax.sharding import PartitionSpec as P

HD = 128
EPSILON = 1e-06
FLOOR = -1e30


def modulated_norm(states, shift, scale):
    values = states.astype(jnp.float32)
    center = jnp.mean(values, axis=-1, keepdims=True)
    spread = jnp.mean(jnp.square(values - center), axis=-1, keepdims=True)
    return ((values - center) * lax.rsqrt(spread + EPSILON) * (1.0 + scale) + shift).astype(
        jnp.bfloat16
    )


def absorb(carry, keys, values, first, queries, limits):
    peak, weight_sum, numer = carry
    videos_here = keys.shape[0]
    count = keys.shape[1]
    heads_here = queries.shape[2]
    head_size = queries.shape[3]
    key_heads = keys.reshape(videos_here, count, heads_here, head_size)
    value_heads = values.reshape(videos_here, count, heads_here, head_size)
    scores = jnp.einsum(
        "vqhd,vkhd->vhqk", queries, key_heads, preferred_element_type=jnp.float32
    ) * head_size ** (-0.5)
    position = first + jnp.arange(count, dtype=jnp.int32)
    valid = (position[None, :] < limits[:, None])[:, None, None, :]
    scores = jnp.where(valid, scores, FLOOR)
    new_peak = jnp.maximum(peak, jnp.max(scores, axis=-1))
    factor = jnp.exp(peak - new_peak)
    probs = jnp.exp(scores - new_peak[..., None]) * valid.astype(jnp.float32)
    weight_sum = weight_sum * factor + jnp.sum(probs, axis=-1)
    numer = numer * factor[..., None] + jnp.einsum(
        "vhqk,vkhd->vhqd",
        probs.astype(jnp.bfloat16),
        value_heads,
        preferred_element_type=jnp.float32,
    )
    return (new_peak, weight_sum, numer)


def body(hidden_states, modulation, w_qkv, w_out, lengths):
    videos_here = hidden_states.shape[0]
    width = hidden_states.shape[2]
    shift = modulation[:, 0][:, None, :]
    scale = modulation[:, 1][:, None, :]
    gate = modulation[:, 2][:, None, :]
    normed = modulated_norm(hidden_states, shift, scale)
    tile_rows = lax.all_gather(normed, "wcol", axis=1, tiled=True)
    tile_len = tile_rows.shape[1]
    local_cols = w_qkv.shape[2]
    flat_rows = tile_rows.reshape(videos_here * tile_len, width)
    piece = lax.all_gather(w_qkv, "wrow", axis=0, tiled=True)
    mixed = jnp.dot(
        flat_rows, piece.reshape(piece.shape[0], 3 * local_cols), preferred_element_type=jnp.float32
    )
    mixed = mixed.reshape(videos_here, tile_len, 3 * local_cols)
    mixed = mixed.astype(jnp.bfloat16).reshape(videos_here, tile_len, 3, local_cols)
    heads_here = local_cols // HD
    queries = mixed[:, :, 0].reshape(videos_here, tile_len, heads_here, HD)
    keys = mixed[:, :, 1]
    values = mixed[:, :, 2]
    start_peak = jnp.full((videos_here, heads_here, tile_len), FLOOR, jnp.float32)
    start_sum = jnp.zeros((videos_here, heads_here, tile_len), jnp.float32)
    start_numer = jnp.zeros((videos_here, heads_here, tile_len, HD), jnp.float32)
    key_piece = lax.all_gather(keys, "patch", axis=1, tiled=True)
    value_piece = lax.all_gather(values, "patch", axis=1, tiled=True)
    count = key_piece.shape[1]
    block_len = 512

    def one_block(index, inner):
        offset = index * block_len
        key_block = lax.dynamic_slice_in_dim(key_piece, offset, block_len, 1)
        value_block = lax.dynamic_slice_in_dim(value_piece, offset, block_len, 1)
        return absorb(inner, key_block, value_block, offset, queries, lengths)

    peak, weight_sum, numer = lax.fori_loop(
        0, count // block_len, one_block, (start_peak, start_sum, start_numer)
    )
    attended = (numer / weight_sum[..., None]).astype(jnp.bfloat16)
    attended = jnp.transpose(attended, (0, 2, 1, 3)).reshape(videos_here * tile_len, local_cols)
    partial_out = jnp.dot(
        attended,
        lax.all_gather(w_out, "wrow", axis=1, tiled=True),
        preferred_element_type=jnp.float32,
    )
    partial_out = partial_out.reshape(videos_here, tile_len, width)
    out_proj = lax.psum_scatter(
        partial_out.astype(jnp.bfloat16), "wcol", scatter_dimension=1, tiled=True
    ).astype(jnp.float32)
    return (hidden_states.astype(jnp.float32) + gate * out_proj).astype(jnp.bfloat16)


def solution(mesh):
    placed = (
        P("wrow", ("patch", "wcol"), None),
        P("wrow", None, None),
        P("wrow", None, "wcol"),
        P("wcol", "wrow"),
        P("wrow"),
    )
    return jax.shard_map(
        body,
        mesh=mesh,
        in_specs=placed,
        out_specs=P("wrow", ("patch", "wcol"), None),
        check_vma=False,
    )
```

profile of v0, /device:TPU:2, one launch (start us, length us, event | category | flops | bytes accessed | tf_op | source)
XLA Modules:
  0.0 490.6 jit_solution(7066353537932086624)
XLA Ops:
  6.5 1.4 slice_reduce_fusion.1
  7.9 1.1 convert_reduce_fusion
  9.0 1.2 fusion.21
  10.3 2.1 fusion.24
  12.4 2.3 copy.12
  14.8 29.8 %all-gather.8.cloned.1.call-done = bf16[1,512,1536]{2,1,0:T(8,128)(2,1)} async-done(((bf16[1,128,1536]{2,1,0:T(8,128)(2,1)}), bf16[1,512,1536]{2,1,0:T(8,128)(2,1)}) %all-gather.8.cloned.1.call-update) | async-done | bytes 1572880 | tf_op jit(solution)/shard_map/all_gather | solution.py:54
  44.6 45.2 %all-gather.10.cloned.1.call-done = bf16[1536,3,384]{0,2,1:T(8,128)(2,1)} async-done(((bf16[384,3,384]{0,2,1:T(8,128)(2,1)}), bf16[1536,3,384]{0,2,1:T(8,128)(2,1)}) %all-gather.10.cloned.1.call-update) | async-done | bytes 3538960 | tf_op jit(solution)/shard_map/all_gather | solution.py:58
  89.8 4.7 convolution_convert_fusion
  95.2 1.0 fusion.27
  97.7 103.0 %all-gather.14.cloned.1.call-done = bf16[1,8192,1,384]{1,3,2,0:T(8,128)(2,1)} async-done(((bf16[1,512,1,384]{1,3,2,0:T(8,128)(2,1)}), bf16[1,8192,1,384]{1,3,2,0:T(8,128)(2,1)}) %all-gather.14.cloned.1.call-update) | async-done | bytes 6291472 | tf_op jit(solution)/shard_map/all_gather | solution.py:71
  200.7 104.5 %all-gather.16.cloned.1.call-done = bf16[1,8192,1,384]{1,3,2,0:T(8,128)(2,1)} async-done(((bf16[1,512,1,384]{1,3,2,0:T(8,128)(2,1)}), bf16[1,8192,1,384]{1,3,2,0:T(8,128)(2,1)}) %all-gather.16.cloned.1.call-update) | async-done | bytes 6291472 | tf_op jit(solution)/shard_map/all_gather | solution.py:72
  305.2 143.9 %while.18 = (s32[]{:T(128)}, f32[1,3,512]{2,1,0:T(4,128)S(1)}, f32[1,3,512]{2,1,0:T(4,128)}, f32[1,3,512,128]{3,2,1,0:T(8,128)}, s32[1]{0:T(128)}, /*index=5*/bf...) while((s32[]{:T(128)}, f32[1,3,512]{2,1,0:T(4,128)S(1)}, ...), condition=%wide.region_5.6_spmd.clone, body=%wide.region_2.5_spmd.clone.sunk | while | flops 413477376 | bytes 13930823 | solution.py:82
  305.2 1.9 constant_dynamic-slice_fusion.3
  307.2 1.2 fusion.43
  309.3 3.2 fusion.46
  314.0 1.9 constant_dynamic-slice_fusion.3
  315.9 1.2 fusion.43
  318.0 3.5 fusion.46
  323.0 1.9 constant_dynamic-slice_fusion.3
  325.0 1.2 fusion.43
  327.1 3.4 fusion.46
  332.0 1.9 constant_dynamic-slice_fusion.3
  334.0 1.2 fusion.43
  336.1 3.4 fusion.46
  341.1 1.9 constant_dynamic-slice_fusion.3
  343.0 1.2 fusion.43
  345.1 3.4 fusion.46
  350.1 1.9 constant_dynamic-slice_fusion.3
  352.0 1.2 fusion.43
  354.1 3.4 fusion.46
  359.1 1.9 constant_dynamic-slice_fusion.3
  361.0 1.2 fusion.43
  363.1 3.4 fusion.46
  368.1 1.9 constant_dynamic-slice_fusion.3
  370.0 1.2 fusion.43
  372.1 3.4 fusion.46
  377.1 1.9 constant_dynamic-slice_fusion.3
  379.0 1.2 fusion.43
  381.1 3.4 fusion.46
  386.1 1.9 constant_dynamic-slice_fusion.3
  388.0 1.2 fusion.43
  390.1 3.4 fusion.46
  395.1 1.9 constant_dynamic-slice_fusion.3
  397.0 1.2 fusion.43
  399.2 3.4 fusion.46
  404.1 1.9 constant_dynamic-slice_fusion.3
  406.0 1.2 fusion.43
  408.2 3.4 fusion.46
  413.1 1.9 constant_dynamic-slice_fusion.3
  415.1 1.2 fusion.43
  417.2 3.4 fusion.46
  422.2 1.9 constant_dynamic-slice_fusion.3
  424.1 1.2 fusion.43
  426.2 3.4 fusion.46
  431.2 1.9 constant_dynamic-slice_fusion.3
  433.1 1.2 fusion.43
  435.2 3.4 fusion.46
  440.2 1.9 constant_dynamic-slice_fusion.3
  442.1 1.2 fusion.43
  444.2 3.4 fusion.46
  449.2 1.4 copy.15
  451.5 3.4 fusion.17
  454.9 27.0 %reduce-scatter.2.cloned.1.call-done = bf16[1,128,1536]{2,1,0:T(8,128)(2,1)} async-done(((bf16[1,512,1536]{2,1,0:T(8,128)(2,1)}), bf16[1,128,1536]{2,1,0:T(8,128)(2,1)}) %reduce-scatter.2.cloned.1.call-update) | async-done | bytes 393232 | tf_op jit(solution)/shard_map/reduce_scatter | solution.py:93
  481.9 1.9 fusion.25
  (265 shorter events, 40.2 us)
Async XLA Ops:
  6.5 38.1 %all-gather.8.cloned.1.call-start = ((), (), s32[]{:S(2)}) async-start(), calls=%async_computation.1 | async-start | bytes 1966080 | tf_op jit(solution)/shard_map/all_gather | solution.py:54
  12.4 77.4 %all-gather.10.cloned.1.call-start = ((), (), s32[]{:S(2)}) async-start(), calls=%async_computation.2 | async-start | bytes 4423680 | tf_op jit(solution)/shard_map/all_gather | solution.py:58
  14.7 186.0 %all-gather.14.cloned.1.call-start = ((), (), s32[]{:S(2)}) async-start(), calls=%async_computation.5 | async-start | bytes 6684672 | tf_op jit(solution)/shard_map/all_gather | solution.py:71
  96.2 209.0 %all-gather.16.cloned.1.call-start = ((), (), s32[]{:S(2)}) async-start(), calls=%async_computation.6 | async-start | bytes 6684672 | tf_op jit(solution)/shard_map/all_gather | solution.py:72
  96.8 354.7 %all-gather.12.cloned.1.call-start = ((), (), s32[]{:S(2)}) async-start(), calls=%async_computation.3 | async-start | bytes 1474560 | tf_op jit(solution)/shard_map/all_gather | solution.py:89
  97.4 384.6 %reduce-scatter.2.cloned.1.call-start = ((), (), s32[]{:S(2)}) async-start(), calls=%async_computation.4 | async-start | bytes 1966080 | tf_op jit(solution)/shard_map/reduce_scatter | solution.py:93
  309.2 3.2 copy-start.3
  309.3 3.2 copy-start.5
  312.5 0.9 copy-start.1
  317.1 0.8 copy-start.4
  318.0 3.5 copy-start.3
  318.0 3.5 copy-start.5
  321.5 0.9 copy-start.1
  327.0 3.5 copy-start.3
  327.1 3.5 copy-start.5
  330.5 0.9 copy-start.1
  335.2 0.8 copy-start.4
  336.1 3.5 copy-start.3
  336.1 3.5 copy-start.5
  339.5 0.9 copy-start.1
  344.2 0.8 copy-start.4
  345.1 3.5 copy-start.3
  345.1 3.5 copy-start.5
  348.5 0.9 copy-start.1
  353.2 0.8 copy-start.4
  354.1 3.5 copy-start.3
  354.1 3.5 copy-start.5
  357.6 0.9 copy-start.1
  362.2 0.8 copy-start.4
  363.1 3.5 copy-start.3
  363.1 3.5 copy-start.5
  366.6 0.9 copy-start.1
  371.2 0.8 copy-start.4
  372.1 3.5 copy-start.3
  372.1 3.5 copy-start.5
  375.6 0.9 copy-start.1
  381.1 3.5 copy-start.3
  381.1 3.5 copy-start.5
  384.6 0.9 copy-start.1
  389.3 0.8 copy-start.4
  390.1 3.5 copy-start.3
  390.1 3.5 copy-start.5
  393.6 0.9 copy-start.1
  399.1 3.5 copy-start.3
  399.1 3.5 copy-start.5
  402.6 0.9 copy-start.1
  408.1 3.5 copy-start.3
  408.2 3.5 copy-start.5
  411.6 0.9 copy-start.1
  417.2 3.5 copy-start.3
  417.2 3.5 copy-start.5
  420.6 0.9 copy-start.1
  425.3 0.8 copy-start.4
  426.2 3.5 copy-start.3
  426.2 3.5 copy-start.5
  429.6 0.9 copy-start.1
  435.2 3.5 copy-start.3
  435.2 3.5 copy-start.5
  438.6 0.9 copy-start.1
  444.2 3.5 copy-start.3
  444.2 3.5 copy-start.5
  447.7 0.9 copy-start.1
  450.6 31.3 %copy-start = (bf16[1,128,1536]{2,1,0:T(8,128)(2,1)S(1)}, bf16[1,128,1536]{2,1,0:T(8,128)(2,1)}, u32[]{:S(2)}) copy-start(bf16[1,128,1536]{2,1,0:T(8,128)(2,1)} %param.7) | copy-start | bytes 1179652
  450.6 31.3 %copy-start.6 = (f32[1536]{0:T(1024)S(1)}, f32[1536]{0:T(1024)}, u32[]{:S(2)}) copy-start(f32[1536]{0:T(1024)} %get-tuple-element.182) | copy-start | bytes 18436
  (24 other events, 16.1 us)
Sparse Core Ops, SparseCore 0:
  12.5 32.0 all-gather.7
  46.4 43.3 all-gather.9
  96.3 104.3 all-gather.13
  203.0 102.2 all-gather.15
  306.9 22.7 all-gather.11
  455.0 26.8 reduce-scatter.1
where the time goes:
time: 492 us; the launch traced here: 491 us
  waiting for transfers between devices  311 us (63%)
  matrix products  76 us (15%)
  local copies, waits for them, and re-layouts  45.7 us (9%)
  other arithmetic  43.1 us (9%)
  between operations  13.6 us (3%)
    all_gather x1, waiting for transfers between devices, body(): value_piece = lax.all_gather(values, 'patch', axis=1, tiled=True)  105 us
    all_gather x1, waiting for transfers between devices, body(): key_piece = lax.all_gather(keys, 'patch', axis=1, tiled=True)  103 us
    dot_general x16, matrix products, absorb(): jnp.einsum('vhqk,vkhd->vhqd', probs.astype(jnp.bfloat16), value_heads, pr...  54.9 us
    all_gather x1, waiting for transfers between devices, body(): piece = lax.all_gather(w_qkv, 'wrow', axis=0, tiled=True)  45.2 us
    dynamic_slice x16, local copies, waits for them, and re-layouts, one_block(): value_block = lax.dynamic_slice_in_dim(value_piece, offset, block_len, 1)  30.6 us
    all_gather x1, waiting for transfers between devices, body(): tile_rows = lax.all_gather(normed, 'wcol', axis=1, tiled=True)  29.8 us
    reduce_scatter x1, waiting for transfers between devices, body(): lax.psum_scatter(partial_out.astype(jnp.bfloat16), 'wcol', scatter_dimens...  27 us
    convert_element_type x16, other arithmetic, absorb(): probs = jnp.exp(scores - new_peak[..., None]) * valid.astype(jnp.float32)  19.9 us
  transfers between devices with their start and end apart: 6, of which 5 were waited for; matrix products, arithmetic and copies ran while one was open for 28% of the time, Pallas kernels for 0%

commit v1 on v0

--- a/solution.py
+++ b/solution.py
@@ -51,7 +51,12 @@
     scale = modulation[:, 1][:, None, :]
     gate = modulation[:, 2][:, None, :]
     normed = modulated_norm(hidden_states, shift, scale)
-    tile_rows = lax.all_gather(normed, "wcol", axis=1, tiled=True)
+    ring = [normed]
+    for hop in range(3):
+        ring.append(lax.ppermute(ring[-1], "wcol", [(dev, (dev + 1) % 4) for dev in range(4)]))
+    tile_rows = jnp.roll(
+        jnp.concatenate(ring[::-1], axis=1), (lax.axis_index("wcol") + 1) * ring[0].shape[1], axis=1
+    )
     tile_len = tile_rows.shape[1]
     local_cols = w_qkv.shape[2]
     flat_rows = tile_rows.reshape(videos_here * tile_len, width)

time: 492 us -> 456 us (0.927)
  waiting for transfers between devices: 311 us -> 270 us
    all_gather x1, waiting for transfers between devices: 45.2 us -> 2.84 us  [body(): piece = lax.all_gather(w_qkv, 'wrow', axis=0, tiled=True)]
    ppermute x0 -> x3, waiting for transfers between devices: none -> 31.9 us  [body(): lax.ppermute(ring[-1], 'wcol', [(dev, (dev + 1) % 4) for dev in range(4)])]
    all_gather x1 -> x0, waiting for transfers between devices: 29.8 us -> none  [body(): tile_rows = lax.all_gather(normed, 'wcol', axis=1, tiled=True)]
  transfers between devices with their start and end apart: 6 -> 8, of which waited for: 5 -> 7; matrix products, arithmetic and copies ran while one was open for 28% -> 32% of each run, Pallas kernels for 0% -> 0%
where the time goes in v1:
time: 456 us; the launch traced here: 455 us
  waiting for transfers between devices  270 us (59%)
  matrix products  76.1 us (17%)
  local copies, waits for them, and re-layouts  50.4 us (11%)
  other arithmetic  41.4 us (9%)
  between operations  13.2 us (3%)
    all_gather x1, waiting for transfers between devices, body(): value_piece = lax.all_gather(values, 'patch', axis=1, tiled=True)  105 us
    all_gather x1, waiting for transfers between devices, body(): key_piece = lax.all_gather(keys, 'patch', axis=1, tiled=True)  103 us
    dot_general x16, matrix products, absorb(): jnp.einsum('vhqk,vkhd->vhqd', probs.astype(jnp.bfloat16), value_heads, pr...  55 us
    ppermute x3, waiting for transfers between devices, body(): lax.ppermute(ring[-1], 'wcol', [(dev, (dev + 1) % 4) for dev in range(4)])  31.9 us
    dynamic_slice x16, local copies, waits for them, and re-layouts, one_block(): value_block = lax.dynamic_slice_in_dim(value_piece, offset, block_len, 1)  30.6 us
    reduce_scatter x1, waiting for transfers between devices, body(): lax.psum_scatter(partial_out.astype(jnp.bfloat16), 'wcol', scatter_dimens...  26.9 us
    convert_element_type x16, other arithmetic, absorb(): probs = jnp.exp(scores - new_peak[..., None]) * valid.astype(jnp.float32)  18.8 us
    reduce_sum x16, other arithmetic, absorb(): weight_sum = weight_sum * factor + jnp.sum(probs, axis=-1)  14.2 us
  transfers between devices with their start and end apart: 8, of which 7 were waited for; matrix products, arithmetic and copies ran while one was open for 32% of the time, Pallas kernels for 0%

profile of v1, /device:TPU:2, one launch (start us, length us, event | category | flops | bytes accessed | tf_op | source)
XLA Modules:
  0.0 455.1 jit_solution(9167025986205443837)
XLA Ops:
  6.5 2.3 copy.12
  8.9 1.4 slice_reduce_fusion.1
  10.3 1.1 convert_reduce_fusion
  12.0 1.7 collective-permute-start
  13.7 10.6 %collective-permute-done = bf16[1,128,1536]{2,1,0:T(8,128)(2,1)S(1)} collective-permute-done((bf16[1,128,1536]{2,1,0:T(8,128)(2,1)S(1)}, bf16[1,128,1536]{2,1,0:T(8,128)(2,1)S(1)}, u32[]{:S(2)}, u32[]{:S(2)}) %collective-permute-start) | collective-permute-done | bytes 393248 | tf_op jit(solution)/shard_map/ppermute | solution.py:56
  24.5 11.0 %collective-permute-done.1 = bf16[1,128,1536]{2,1,0:T(8,128)(2,1)S(1)} collective-permute-done((bf16[1,128,1536]{2,1,0:T(8,128)(2,1)S(1)}, bf16[1,128,1536]{2,1,0:T(8,128)(2,1)S(1)}, u32[]{:S(2)}, u32[]{:S(2)}) %collective-permute-start.1) | collective-permute-done | bytes 393248 | tf_op jit(solution)/shard_map/ppermute | solution.py:56
  35.5 10.3 %collective-permute-done.2 = bf16[1,128,1536]{2,1,0:T(8,128)(2,1)S(1)} collective-permute-done((bf16[1,128,1536]{2,1,0:T(8,128)(2,1)S(1)}, bf16[1,128,1536]{2,1,0:T(8,128)(2,1)S(1)}, u32[]{:S(2)}, u32[]{:S(2)}) %collective-permute-start.2) | collective-permute-done | bytes 393248 | tf_op jit(solution)/shard_map/ppermute | solution.py:56
  52.6 2.8 all-gather.7.cloned.1.call-done
  55.5 4.7 %convolution_convert_fusion = bf16[512,1152]{1,0:T(8,128)(2,1)S(1)} fusion(bf16[1536,1152]{0,1:T(8,128)(2,1)} %bitcast.91, bf16[1,1024,1536]{2,1,0:T(8,128)(2,1)} %constant_dynamic-update-slice_fusion, s32[]{:T(128)S(6)} %select_n.34), kind=kOutput, calls=%fused_computation.23 | convolution fusion | flops 1812529152 | bytes 6291460 | tf_op jit(solution)/shard_map/dot_general | solution.py:64
  63.4 102.9 %all-gather.11.cloned.1.call-done = bf16[1,8192,1,384]{1,3,2,0:T(8,128)(2,1)} async-done(((bf16[1,512,1,384]{1,3,2,0:T(8,128)(2,1)}), bf16[1,8192,1,384]{1,3,2,0:T(8,128)(2,1)}) %all-gather.11.cloned.1.call-update) | async-done | bytes 6291472 | tf_op jit(solution)/shard_map/all_gather | solution.py:76
  166.3 104.7 %all-gather.13.cloned.1.call-done = bf16[1,8192,1,384]{1,3,2,0:T(8,128)(2,1)} async-done(((bf16[1,512,1,384]{1,3,2,0:T(8,128)(2,1)}), bf16[1,8192,1,384]{1,3,2,0:T(8,128)(2,1)}) %all-gather.13.cloned.1.call-update) | async-done | bytes 6291472 | tf_op jit(solution)/shard_map/all_gather | solution.py:77
  271.0 143.1 %while.18 = (s32[]{:T(128)}, f32[1,3,512]{2,1,0:T(4,128)S(1)}, f32[1,3,512]{2,1,0:T(4,128)}, f32[1,3,512,128]{3,2,1,0:T(8,128)}, s32[1]{0:T(128)}, /*index=5*/bf...) while((s32[]{:T(128)}, f32[1,3,512]{2,1,0:T(4,128)S(1)}, ...), condition=%wide.region_5.6_spmd.clone, body=%wide.region_2.5_spmd.clone.sunk | while | flops 413477376 | bytes 13930823 | solution.py:87
  271.0 1.9 constant_dynamic-slice_fusion.3
  272.9 1.2 fusion.45
  275.0 3.2 fusion.48
  279.7 1.9 constant_dynamic-slice_fusion.3
  281.6 1.2 fusion.45
  283.7 3.5 fusion.48
  288.7 1.9 constant_dynamic-slice_fusion.3
  290.7 1.2 fusion.45
  292.7 3.4 fusion.48
  297.7 1.9 constant_dynamic-slice_fusion.3
  299.6 1.2 fusion.45
  301.7 3.4 fusion.48
  306.7 1.9 constant_dynamic-slice_fusion.3
  308.6 1.2 fusion.45
  310.6 3.4 fusion.48
  315.6 1.9 constant_dynamic-slice_fusion.3
  317.5 1.2 fusion.45
  319.6 3.4 fusion.48
  324.6 1.9 constant_dynamic-slice_fusion.3
  326.5 1.2 fusion.45
  328.5 3.4 fusion.48
  333.5 1.9 constant_dynamic-slice_fusion.3
  335.4 1.2 fusion.45
  337.5 3.4 fusion.48
  342.5 1.9 constant_dynamic-slice_fusion.3
  344.4 1.2 fusion.45
  346.4 3.4 fusion.48
  351.4 1.9 constant_dynamic-slice_fusion.3
  353.3 1.2 fusion.45
  355.4 3.4 fusion.48
  360.4 1.9 constant_dynamic-slice_fusion.3
  362.3 1.2 fusion.45
  364.3 3.4 fusion.48
  369.3 1.9 constant_dynamic-slice_fusion.3
  371.2 1.2 fusion.45
  373.3 3.4 fusion.48
  378.3 1.9 constant_dynamic-slice_fusion.3
  380.2 1.2 fusion.45
  382.2 3.4 fusion.48
  387.2 1.9 constant_dynamic-slice_fusion.3
  389.1 1.2 fusion.45
  391.2 3.4 fusion.48
  396.2 1.9 constant_dynamic-slice_fusion.3
  398.1 1.2 fusion.45
  400.1 3.4 fusion.48
  405.1 1.9 constant_dynamic-slice_fusion.3
  407.0 1.2 fusion.45
  409.1 3.4 fusion.48
  414.1 1.4 copy.15
  416.4 3.4 fusion.17
  419.8 26.9 %reduce-scatter.2.cloned.1.call-done = bf16[1,128,1536]{2,1,0:T(8,128)(2,1)} async-done(((bf16[1,512,1536]{2,1,0:T(8,128)(2,1)}), bf16[1,128,1536]{2,1,0:T(8,128)(2,1)}) %reduce-scatter.2.cloned.1.call-update) | async-done | bytes 393232 | tf_op jit(solution)/shard_map/reduce_scatter | solution.py:98
  446.7 1.9 fusion.26
  (278 shorter events, 49.0 us)
Async XLA Ops:
  6.5 4.9 %copy-start = (bf16[1,128,1536]{2,1,0:T(8,128)(2,1)S(1)}, bf16[1,128,1536]{2,1,0:T(8,128)(2,1)}, u32[]{:S(2)}) copy-start(bf16[1,128,1536]{2,1,0:T(8,128)(2,1)} %param.7) | copy-start | bytes 1179652
  6.5 48.9 %all-gather.7.cloned.1.call-start = ((), (), s32[]{:S(2)}) async-start(), calls=%async_computation.1 | async-start | bytes 4423680 | tf_op jit(solution)/shard_map/all_gather | solution.py:63
  8.9 157.5 %all-gather.11.cloned.1.call-start = ((), (), s32[]{:S(2)}) async-start(), calls=%async_computation.4 | async-start | bytes 6684672 | tf_op jit(solution)/shard_map/all_gather | solution.py:76
  12.0 12.2 %collective-permute-start = (bf16[1,128,1536]{2,1,0:T(8,128)(2,1)S(1)}, bf16[1,128,1536]{2,1,0:T(8,128)(2,1)S(1)}, u32[]{:S(2)}, u32[]{:S(2)}) collective-permute-start(bf16[1,128,1536]{2,1,0:T(8,128)(2,1)S(1)} %fusion.25), channel_id=1, source_target_pairs={{0,1},{1,2},{2,3},{3,0},{4,5},{5,6},{6,7},{7,4},{8,9},{9,10},{10,1... | collective-permute-start | bytes 1179656 | tf_op jit(solution)/shard_map/ppermute | solution.py:56
  24.2 11.3 %collective-permute-start.1 = (bf16[1,128,1536]{2,1,0:T(8,128)(2,1)S(1)}, bf16[1,128,1536]{2,1,0:T(8,128)(2,1)S(1)}, u32[]{:S(2)}, u32[]{:S(2)}) collective-permute-start(bf16[1,128,1536]{2,1,0:T(8,128)(2,1)S(1)} %collective-permute-done), channel_id=1, source_target_pairs={{0,1},{1,2},{2,3},{3,0},{4,5},{5,6},{6,7},{7,4},{8,9},{9,10},{10,1... | collective-permute-start | bytes 1179656 | tf_op jit(solution)/shard_map/ppermute | solution.py:56
  35.5 10.3 %collective-permute-start.2 = (bf16[1,128,1536]{2,1,0:T(8,128)(2,1)S(1)}, bf16[1,128,1536]{2,1,0:T(8,128)(2,1)S(1)}, u32[]{:S(2)}, u32[]{:S(2)}) collective-permute-start(bf16[1,128,1536]{2,1,0:T(8,128)(2,1)S(1)} %collective-permute-done.1), channel_id=1, source_target_pairs={{0,1},{1,2},{2,3},{3,0},{4,5},{5,6},{6,7},{7,4},{8,9},{9,10},{10,1... | collective-permute-start | bytes 1179656 | tf_op jit(solution)/shard_map/ppermute | solution.py:56
  61.8 209.2 %all-gather.13.cloned.1.call-start = ((), (), s32[]{:S(2)}) async-start(), calls=%async_computation.5 | async-start | bytes 6684672 | tf_op jit(solution)/shard_map/all_gather | solution.py:77
  62.6 353.8 %all-gather.9.cloned.1.call-start = ((), (), s32[]{:S(2)}) async-start(), calls=%async_computation.2 | async-start | bytes 1474560 | tf_op jit(solution)/shard_map/all_gather | solution.py:94
  63.1 383.6 %reduce-scatter.2.cloned.1.call-start = ((), (), s32[]{:S(2)}) async-start(), calls=%async_computation.3 | async-start | bytes 1966080 | tf_op jit(solution)/shard_map/reduce_scatter | solution.py:98
  275.0 3.2 copy-start.4
  275.0 3.2 copy-start.6
  278.2 0.9 copy-start.2
  283.7 3.6 copy-start.4
  283.7 3.6 copy-start.6
  287.2 0.9 copy-start.2
  292.7 3.5 copy-start.4
  292.7 3.5 copy-start.6
  296.2 0.9 copy-start.2
  301.6 3.5 copy-start.4
  301.7 3.5 copy-start.6
  305.1 0.9 copy-start.2
  310.6 3.5 copy-start.4
  310.6 3.5 copy-start.6
  314.1 0.9 copy-start.2
  318.7 0.8 copy-start.5
  319.6 3.5 copy-start.4
  319.6 3.5 copy-start.6
  323.0 0.9 copy-start.2
  327.7 0.8 copy-start.5
  328.5 3.5 copy-start.4
  328.5 3.5 copy-start.6
  332.0 0.9 copy-start.2
  336.6 0.8 copy-start.5
  337.5 3.5 copy-start.4
  337.5 3.5 copy-start.6
  340.9 0.9 copy-start.2
  345.6 0.8 copy-start.5
  346.4 3.5 copy-start.4
  346.4 3.5 copy-start.6
  349.9 0.9 copy-start.2
  354.5 0.8 copy-start.5
  355.4 3.5 copy-start.4
  355.4 3.5 copy-start.6
  358.8 0.9 copy-start.2
  364.3 3.5 copy-start.4
  364.3 3.5 copy-start.6
  367.8 0.9 copy-start.2
  373.3 3.5 copy-start.4
  373.3 3.5 copy-start.6
  376.7 0.9 copy-start.2
  382.2 3.5 copy-start.4
  382.2 3.5 copy-start.6
  385.7 0.9 copy-start.2
  391.2 3.5 copy-start.4
  391.2 3.5 copy-start.6
  394.6 0.9 copy-start.2
  400.1 3.5 copy-start.4
  400.1 3.5 copy-start.6
  403.6 0.9 copy-start.2
  409.1 3.5 copy-start.4
  409.1 3.5 copy-start.6
  412.5 0.9 copy-start.2
  415.5 31.3 %copy-start.1 = (bf16[1,128,1536]{2,1,0:T(8,128)(2,1)S(1)}, bf16[1,128,1536]{2,1,0:T(8,128)(2,1)}, u32[]{:S(2)}) copy-start(bf16[1,128,1536]{2,1,0:T(8,128)(2,1)} %param.7) | copy-start | bytes 1179652
  415.5 31.3 %copy-start.7 = (f32[1536]{0:T(1024)S(1)}, f32[1536]{0:T(1024)}, u32[]{:S(2)}) copy-start(f32[1536]{0:T(1024)} %get-tuple-element.182) | copy-start | bytes 18436
  (27 other events, 18.6 us)
Sparse Core Ops, SparseCore 0:
  9.2 46.2 all-gather.6
  61.9 104.3 all-gather.10
  168.7 102.2 all-gather.12
  272.7 22.7 all-gather.8
  419.9 26.7 reduce-scatter.1
